TPU v7x, 512 devices: a whole 4x8x8 slice. The times are simulated.
512 devices in a mesh: sub: 256 (over z, y, x), sep: 2 (over core).
Axes of the slice: x: 4, y: 8, z: 8, core: 2. Of those that a mesh axis runs over, the one named last changes fastest.
Arguments:
- sources: bfloat16 [256, 2, 768, 256], P('sub', 'sep'), may hold values from -6 to 6
- inner_inv: bfloat16 [256, 2, 768, 768], P('sub', 'sep'), as said below
- coupling: bfloat16 [256, 2, 512, 768], P('sub', 'sep'), may hold values from -0.0546875 to 0.0546875
- boundary_map: int32 [256, 2, 512], P('sub', 'sep'), may hold values from 0 to 479, as said below
- sep_inv_0: bfloat16 [256, 64, 64], P('sub', 'sep'), as said below
- sep_inv_1: bfloat16 [256, 128, 128], P('sub', 'sep'), as said below
- sep_inv_2: bfloat16 [256, 256, 256], P('sub', 'sep'), as said below
- sep_inv_3: bfloat16 [256, 512, 512], P('sub', 'sep'), as said below
- sep_couple_0: bfloat16 [256, 128, 64], P('sub', 'sep'), as said below
- sep_couple_1: bfloat16 [256, 256, 128], P('sub', 'sep'), as said below
- sep_couple_2: bfloat16 [256, 512, 256], P('sub', 'sep'), as said below
Outputs:
- inner_solution: bfloat16 [256, 2, 768, 256], P('sub', 'sep')
- sep_solution: bfloat16 [256, 2, 480, 256], P('sub', 'sep')
Inputs may be any that keep to these rules, and one draw needn't show every extreme that they name: `boundary_map`: an entry m with (2^l - 1) * 32 <= m < (2^(l+1) - 1) * 32 names row m - (2^l - 1) * 32 of the leaf's own strip in the level-l separator above its subdomain. Every inner_inv[s, p] is lower triangular with a positive diagonal. Every sep_inv_0[s] is lower triangular with a positive diagonal, and equal for all s of one level-0 group. Every sep_inv_1[s] is lower triangular with a positive diagonal, and equal for all s of one level-1 group. Every sep_inv_2[s] is lower triangular with a positive diagonal, and equal for all s of one level-2 group. Every sep_inv_3[s] is lower triangular with a positive diagonal, and equal for all s of one level-3 group. sep_couple_0[s] is equal for all s of one level-0 group. sep_couple_1[s] is equal for all s of one level-1 group. sep_couple_2[s] is equal for all s of one level-2 group.
All inputs are finite; a program needn't handle non-finite values.
Results may differ from a plain program's by a relative error of at most 0.017.
Values may be sent and summed in bfloat16 or wider, within the bound.
A program may use at most 64 MiB of HBM per device.

v0:
```python
import jax
import jax.numpy as jnp
from jax import lax
from jax.sharding import PartitionSpec as P


def joined_along(tiles, dim):
    tiles = jnp.moveaxis(tiles, 0, dim)
    shape = tiles.shape
    return tiles.reshape(*shape[:dim], shape[dim] * shape[dim + 1], *shape[dim + 2 :])


def gather_together(arrays, axis, dims):
    ravelled = jnp.concatenate([a.reshape(-1) for a in arrays])
    lines, at, done = (lax.all_gather(ravelled, axis), 0, [])
    for a, dim in zip(arrays, dims):
        tiles = lines[:, at : at + a.size].reshape(-1, *a.shape)
        done.append(joined_along(tiles, dim))
        at += a.size
    return tuple(done)


def copy_for_each(x, axis):
    devices = lax.axis_size(axis)
    return lax.all_to_all(jnp.broadcast_to(x[None], (devices, *x.shape)), axis, 0, 0, tiled=True)


def gather_directly(x, axis, dim):
    return joined_along(copy_for_each(x, axis), dim)


def swapped(block, axis, stride):
    count = lax.axis_size(axis)
    route = []
    for low in range(count):
        high = low | 1 << stride
        if high != low and high < count:
            route += [(low, high), (high, low)]
    return lax.ppermute(block, axis, route)


def row_fold(matrix, arrived):
    return jnp.dot(matrix, arrived, preferred_element_type=jnp.float32)


def transposed_product(matrix, rows):
    return lax.dot_general(
        matrix, rows, (((0,), (0,)), ((), ())), preferred_element_type=jnp.float32
    )


def local(
    sources,
    inner_inv,
    coupling,
    boundary_map,
    sep_inv_0,
    sep_inv_1,
    sep_inv_2,
    sep_inv_3,
    sep_couple_0,
    sep_couple_1,
    sep_couple_2,
):
    source_rows = sources[0, 0]
    inverse = inner_inv[0, 0]
    couple = coupling[0, 0]
    targets = boundary_map[0, 0]
    separators = [sep_inv_0[0], sep_inv_1[0], sep_inv_2[0], sep_inv_3[0]]
    parents = [sep_couple_0[0], sep_couple_1[0], sep_couple_2[0]]
    levels = len(separators)
    row_sizes = [matrix.shape[0] for matrix in separators]
    total_rows = sum(row_sizes)
    bit_count = lax.axis_size("sub").bit_length() - 1
    gathered = gather_together(
        (
            separators[0],
            separators[1],
            separators[2],
            separators[3],
            parents[0],
            parents[1],
            parents[2],
        ),
        "sep",
        (0, 0, 0, 0, 0, 0, 0),
    )
    full_separator = list(gathered[:4])
    full_parent = list(gathered[4:])
    inner_half = jnp.dot(inverse, source_rows, preferred_element_type=jnp.float32).astype(
        jnp.bfloat16
    )
    boundary_half = jnp.dot(couple, inner_half, preferred_element_type=jnp.float32).astype(
        jnp.bfloat16
    )
    slot_ids = lax.broadcasted_iota(jnp.int32, (total_rows, targets.shape[0]), 0)
    onehot = (slot_ids == targets[None, :]).astype(jnp.bfloat16)
    leaf_rows = jnp.dot(onehot, boundary_half, preferred_element_type=jnp.float32)
    direct = lax.dot_general(
        inverse, inner_half, (((0,), (0,)), ((), ())), preferred_element_type=jnp.float32
    )
    forward_rows = []
    carried = leaf_rows
    for height in range(levels):
        for bit_index in range(2 * height, min(2 * height + 2, bit_count)):
            carried = carried + swapped(carried.astype(jnp.bfloat16), "sub", bit_index).astype(
                carried.dtype
            )
        size = row_sizes[height]
        rhs_rows = carried[:size]
        rhs_half = rhs_rows.astype(jnp.bfloat16)
        solve_solved = row_fold(
            separators[height], lax.all_gather(rhs_half, "sep", axis=0, tiled=True)
        )
        solved = solve_solved.astype(jnp.bfloat16)
        forward_rows.append(solved)
        carried = carried[size:]
        if height < levels - 1:
            child_term = row_fold(parents[height], gather_directly(solved, "sep", 0))
            carried = carried.at[: row_sizes[height + 1]].add(child_term)
    backward_rows = [None] * levels
    full_forward = [None] * levels
    for height in range(levels):
        full_forward[height] = gather_directly(forward_rows[height], "sep", 0)
    full_down = None
    for height in reversed(range(levels)):
        if height == levels - 1:
            full_target = full_forward[height]
        else:
            back_term = transposed_product(full_parent[height], full_down)
            full_target = (full_forward[height].astype(jnp.float32) - back_term).astype(
                jnp.bfloat16
            )
        full_down = transposed_product(full_separator[height], full_target).astype(jnp.bfloat16)
        own_start = lax.axis_index("sep") * row_sizes[height]
        backward_rows[height] = lax.dynamic_slice_in_dim(full_down, own_start, row_sizes[height], 0)
    stacked = jnp.concatenate(backward_rows, axis=0)
    picked = jnp.take(stacked, targets, axis=0)
    lifted = lax.dot_general(
        couple, picked, (((0,), (0,)), ((), ())), preferred_element_type=jnp.float32
    ).astype(jnp.bfloat16)
    correction = lax.dot_general(
        inverse, lifted, (((0,), (0,)), ((), ())), preferred_element_type=jnp.float32
    )
    inner_solution = (direct - correction).astype(jnp.bfloat16)
    return (inner_solution[None, None], stacked[None, None])


def solution(mesh):
    placed = (
        P("sub", "sep", None, None),
        P("sub", "sep", None, None),
        P("sub", "sep", None, None),
        P("sub", "sep", None),
        P("sub", "sep", None),
        P("sub", "sep", None),
        P("sub", "sep", None),
        P("sub", "sep", None),
        P("sub", "sep", None),
        P("sub", "sep", None),
        P("sub", "sep", None),
    )
    return jax.shard_map(
        local,
        mesh=mesh,
        in_specs=placed,
        out_specs=(P("sub", "sep", None, None), P("sub", "sep", None, None)),
        check_vma=False,
    )
```

profile of v0, /device:TPU:1, one launch (start us, length us, event | category | flops | bytes accessed | tf_op | source)
XLA Modules:
  0.0 139.3 jit_solution(10108496748243036208)
XLA Ops:
  0.7 1.2 copy-done
  1.9 1.5 %convolution_convert_fusion.1 = bf16[768,256]{1,0:T(8,128)(2,1)S(1)} fusion(bf16[1,1,768,768]{3,2,1,0:T(8,128)(2,1)S(1)} %copy-done, bf16[1,1,768,256]{3,2,1,0:T(8,128)(2,1)} %param.19), kind=kOutput, calls=%fused_computation.4 | convolution fusion | flops 302186496 | bytes 1966080 | tf_op jit(solution)/shard_map/dot_general | solution.py:90
  3.4 1.4 fusion.52
  4.8 4.1 %collective-permute-start = (bf16[480,256]{1,0:T(8,128)(2,1)}, bf16[480,256]{1,0:T(8,128)(2,1)S(1)}, u32[]{:S(2)}, u32[]{:S(2)}) collective-permute-start(bf16[480,256]{1,0:T(8,128)(2,1)} %get-tuple-element.54), channel_id=1, source_target_pairs={{0,2},{2,0},{4,6},{6,4},{8,10},{10,8},{12,14},{14,12},{16,18},{18,... | collective-permute-start | bytes 737288 | tf_op jit(solution)/shard_map/ppermute | solution.py:39
  9.0 0.9 copy.30
  10.1 2.6 %collective-permute-done = bf16[480,256]{1,0:T(8,128)(2,1)S(1)} collective-permute-done((bf16[480,256]{1,0:T(8,128)(2,1)}, bf16[480,256]{1,0:T(8,128)(2,1)S(1)}, u32[]{:S(2)}, u32[]{:S(2)}) %collective-permute-start) | collective-permute-done | bytes 245792 | tf_op jit(solution)/shard_map/ppermute | solution.py:39
  12.7 0.7 fusion.21
  13.4 6.7 %collective-permute-start.1 = (bf16[480,256]{1,0:T(8,128)(2,1)}, bf16[480,256]{1,0:T(8,128)(2,1)S(1)}, u32[]{:S(2)}, u32[]{:S(2)}) collective-permute-start(bf16[480,256]{1,0:T(8,128)(2,1)} %fusion.21), channel_id=1, source_target_pairs={{0,4},{4,0},{2,6},{6,2},{8,12},{12,8},{10,14},{14,10},{16,20},{20,... | collective-permute-start | bytes 737288 | tf_op jit(solution)/shard_map/ppermute | solution.py:39
  20.3 3.5 %collective-permute-done.1 = bf16[480,256]{1,0:T(8,128)(2,1)S(1)} collective-permute-done((bf16[480,256]{1,0:T(8,128)(2,1)}, bf16[480,256]{1,0:T(8,128)(2,1)S(1)}, u32[]{:S(2)}, u32[]{:S(2)}) %collective-permute-start.1) | collective-permute-done | bytes 245792 | tf_op jit(solution)/shard_map/ppermute | solution.py:39
  24.0 8.2 %all_gather.20 = bf16[64,256]{1,0:T(8,128)(2,1)S(1)} all-gather(bf16[32,256]{1,0:T(8,128)(2,1)S(1)} %slice.140), channel_id=1, replica_groups=mesh['sub'=256,'sep'=2] {'sep'}, dimensions={0}, use_global_device_ids=true | all-gather | bytes 49152 | tf_op jit(solution)/shard_map/all_gather | solution.py:113
  32.2 0.1 fusion.14
  32.4 3.7 %all_to_all.23 = bf16[2,32,256]{2,1,0:T(8,128)(2,1)S(1)} all-to-all(bf16[2,32,256]{2,1,0:T(8,128)(2,1)S(1)} %broadcast_in_dim.20), channel_id=1, replica_groups=mesh['sub'=256,'sep'=2] {'sep'}, dimensions={0} | all-to-all | bytes 65536 | tf_op jit(solution)/shard_map/all_to_all | solution.py:25
  36.1 0.1 fusion.38
  36.3 1.9 %collective-permute-start.2 = (bf16[448,256]{1,0:T(8,128)(2,1)S(1)}, bf16[448,256]{1,0:T(8,128)(2,1)S(1)}, u32[]{:S(2)}, u32[]{:S(2)}) collective-permute-start(bf16[448,256]{1,0:T(8,128)(2,1)S(1)} %convert_element_type.135), channel_id=1, source_target_pairs={{0,8},{8,0},{2,10},{10,2},{4,12},{12,4},{6,14},{14,6},{16,24},{24,... | collective-permute-start | bytes 688136 | tf_op jit(solution)/shard_map/ppermute | solution.py:39
  38.2 6.8 %collective-permute-done.2 = bf16[448,256]{1,0:T(8,128)(2,1)S(1)} collective-permute-done((bf16[448,256]{1,0:T(8,128)(2,1)S(1)}, bf16[448,256]{1,0:T(8,128)(2,1)S(1)}, u32[]{:S(2)}, u32[]{:S(2)}) %collective-permute-start.2) | collective-permute-done | bytes 229408 | tf_op jit(solution)/shard_map/ppermute | solution.py:39
  45.0 1.9 %collective-permute-start.3 = (bf16[448,256]{1,0:T(8,128)(2,1)S(1)}, bf16[448,256]{1,0:T(8,128)(2,1)S(1)}, u32[]{:S(2)}, u32[]{:S(2)}) collective-permute-start(bf16[448,256]{1,0:T(8,128)(2,1)S(1)} %fusion.22), channel_id=1, source_target_pairs={{0,16},{16,0},{2,18},{18,2},{4,20},{20,4},{6,22},{22,6},{8,24},{24... | collective-permute-start | bytes 688136 | tf_op jit(solution)/shard_map/ppermute | solution.py:39
  47.0 13.3 %collective-permute-done.3 = bf16[448,256]{1,0:T(8,128)(2,1)S(1)} collective-permute-done((bf16[448,256]{1,0:T(8,128)(2,1)S(1)}, bf16[448,256]{1,0:T(8,128)(2,1)S(1)}, u32[]{:S(2)}, u32[]{:S(2)}) %collective-permute-start.3) | collective-permute-done | bytes 229408 | tf_op jit(solution)/shard_map/ppermute | solution.py:39
  60.4 2.0 %all_gather.21 = bf16[128,256]{1,0:T(8,128)(2,1)S(1)} all-gather(bf16[64,256]{1,0:T(8,128)(2,1)S(1)} %slice.139), channel_id=1, replica_groups=mesh['sub'=256,'sep'=2] {'sep'}, dimensions={0}, use_global_device_ids=true | all-gather | bytes 98304 | tf_op jit(solution)/shard_map/all_gather | solution.py:113
  62.4 0.1 fusion.12
  62.5 3.8 %all_to_all.24 = bf16[2,64,256]{2,1,0:T(8,128)(2,1)S(1)} all-to-all(bf16[2,64,256]{2,1,0:T(8,128)(2,1)S(1)} %broadcast_in_dim.21), channel_id=1, replica_groups=mesh['sub'=256,'sep'=2] {'sep'}, dimensions={0} | all-to-all | bytes 131072 | tf_op jit(solution)/shard_map/all_to_all | solution.py:25
  66.3 0.1 fusion.31
  66.5 0.5 copy-done.5
  67.0 4.2 %collective-permute-start.4 = (bf16[384,256]{1,0:T(8,128)(2,1)S(1)}, bf16[384,256]{1,0:T(8,128)(2,1)S(1)}, u32[]{:S(2)}, u32[]{:S(2)}) collective-permute-start(bf16[384,256]{1,0:T(8,128)(2,1)S(1)} %convert_element_type.142), channel_id=1, source_target_pairs={{0,32},{32,0},{2,34},{34,2},{4,36},{36,4},{6,38},{38,6},{8,40},{40... | collective-permute-start | bytes 589832 | tf_op jit(solution)/shard_map/ppermute | solution.py:39
  71.2 1.4 %fusion.3 = f32[256,768]{1,0:T(8,128)} fusion(bf16[768,256]{1,0:T(8,128)(2,1)S(1)} %convolution_convert_fusion.1, bf16[1,1,768,768]{3,2,1,0:T(8,128)(2,1)S(1)} %copy-done), kind=kOutput, calls=%fused_computation.9 | convolution fusion | flops 301989888 | bytes 2359296 | tf_op jit(solution)/shard_map/dot_general | solution.py:99
  72.7 10.4 %collective-permute-done.4 = bf16[384,256]{1,0:T(8,128)(2,1)S(1)} collective-permute-done((bf16[384,256]{1,0:T(8,128)(2,1)S(1)}, bf16[384,256]{1,0:T(8,128)(2,1)S(1)}, u32[]{:S(2)}, u32[]{:S(2)}) %collective-permute-start.4) | collective-permute-done | bytes 196640 | tf_op jit(solution)/shard_map/ppermute | solution.py:39
  83.1 2.1 %collective-permute-start.5 = (bf16[384,256]{1,0:T(8,128)(2,1)S(1)}, bf16[384,256]{1,0:T(8,128)(2,1)S(1)}, u32[]{:S(2)}, u32[]{:S(2)}) collective-permute-start(bf16[384,256]{1,0:T(8,128)(2,1)S(1)} %fusion.23), channel_id=1, source_target_pairs={{0,64},{64,0},{2,66},{66,2},{4,68},{68,4},{6,70},{70,6},{8,72},{72... | collective-permute-start | bytes 589832 | tf_op jit(solution)/shard_map/ppermute | solution.py:39
  85.2 2.6 %all-gather = bf16[520192]{0:T(1024)(128)(2,1)S(1)} all-gather(bf16[260096]{0:T(1024)(128)(2,1)S(1)} %constant_dynamic-update-slice_fusion), channel_id=2, replica_groups=mesh['sub'=256,'sep'=2] {'sep'}, dimensions={0}, use_global_device_ids=true | all-gather | bytes 1560576 | tf_op jit(solution)/shard_map/all_gather | solution.py:15
  87.9 3.3 %collective-permute-done.5 = bf16[384,256]{1,0:T(8,128)(2,1)S(1)} collective-permute-done((bf16[384,256]{1,0:T(8,128)(2,1)S(1)}, bf16[384,256]{1,0:T(8,128)(2,1)S(1)}, u32[]{:S(2)}, u32[]{:S(2)}) %collective-permute-start.5) | collective-permute-done | bytes 196640 | tf_op jit(solution)/shard_map/ppermute | solution.py:39
  91.2 2.9 %all_gather.22 = bf16[256,256]{1,0:T(8,128)(2,1)S(1)} all-gather(bf16[128,256]{1,0:T(8,128)(2,1)S(1)} %slice.138), channel_id=1, replica_groups=mesh['sub'=256,'sep'=2] {'sep'}, dimensions={0}, use_global_device_ids=true | all-gather | bytes 196608 | tf_op jit(solution)/shard_map/all_gather | solution.py:113
  94.1 0.2 fusion.10
  94.3 0.1 copy.24
  94.5 3.8 %all_to_all.25 = bf16[2,128,256]{2,1,0:T(8,128)(2,1)S(1)} all-to-all(bf16[2,128,256]{2,1,0:T(8,128)(2,1)S(1)} %broadcast_in_dim.22), channel_id=1, replica_groups=mesh['sub'=256,'sep'=2] {'sep'}, dimensions={0} | all-to-all | bytes 262144 | tf_op jit(solution)/shard_map/all_to_all | solution.py:25
  98.3 0.2 fusion.55
  98.5 2.3 %collective-permute-start.6 = (bf16[256,256]{1,0:T(8,128)(2,1)S(1)}, bf16[256,256]{1,0:T(8,128)(2,1)S(1)}, u32[]{:S(2)}, u32[]{:S(2)}) collective-permute-start(bf16[256,256]{1,0:T(8,128)(2,1)S(1)} %get-tuple-element.56), channel_id=1, source_target_pairs={{0,128},{128,0},{2,130},{130,2},{4,132},{132,4},{6,134},{134,6},{8... | collective-permute-start | bytes 393224 | tf_op jit(solution)/shard_map/ppermute | solution.py:39
  100.9 0.6 compare_select_fusion
  101.5 7.8 %collective-permute-done.6 = bf16[256,256]{1,0:T(8,128)(2,1)S(1)} collective-permute-done((bf16[256,256]{1,0:T(8,128)(2,1)S(1)}, bf16[256,256]{1,0:T(8,128)(2,1)S(1)}, u32[]{:S(2)}, u32[]{:S(2)}) %collective-permute-start.6) | collective-permute-done | bytes 131104 | tf_op jit(solution)/shard_map/ppermute | solution.py:39
  109.3 0.7 fusion.30
  110.0 6.0 %collective-permute-start.7 = (bf16[256,256]{1,0:T(8,128)(2,1)}, bf16[256,256]{1,0:T(8,128)(2,1)}, u32[]{:S(2)}, u32[]{:S(2)}) collective-permute-start(bf16[256,256]{1,0:T(8,128)(2,1)} %fusion.30), channel_id=1, source_target_pairs={{0,256},{256,0},{2,258},{258,2},{4,260},{260,4},{6,262},{262,6},{8... | collective-permute-start | bytes 393224 | tf_op jit(solution)/shard_map/ppermute | solution.py:39
  116.0 0.5 compare_and_fusion
  116.6 0.3 reshape.144
  116.8 0.4 slice.126
  117.2 0.2 slice.125
  117.4 0.7 slice.121
  118.1 0.7 slice.120
  118.8 0.6 slice.115
  119.5 0.6 slice.113
  120.1 0.5 reshape_reshape.27
  120.6 0.2 reshape_reshape.26
  120.7 0.2 copy-done.11
  121.4 0.7 pad_clamp_fusion
  122.0 1.4 %collective-permute-done.7 = bf16[256,256]{1,0:T(8,128)(2,1)} collective-permute-done((bf16[256,256]{1,0:T(8,128)(2,1)}, bf16[256,256]{1,0:T(8,128)(2,1)}, u32[]{:S(2)}, u32[]{:S(2)}) %collective-permute-start.7) | collective-permute-done | bytes 131104 | tf_op jit(solution)/shard_map/ppermute | solution.py:39
  123.5 1.0 add_convert_fusion
  124.5 3.0 %all_gather.23 = bf16[512,256]{1,0:T(8,128)(2,1)S(1)} all-gather(bf16[256,256]{1,0:T(8,128)(2,1)S(1)} %add_convert_fusion), channel_id=1, replica_groups=mesh['sub'=256,'sep'=2] {'sep'}, dimensions={0}, use_global_device_ids=true | all-gather | bytes 393216 | tf_op jit(solution)/shard_map/all_gather | solution.py:113
  127.5 0.3 fusion.8
  127.7 0.1 copy.26
  127.9 4.1 %all_to_all.26 = bf16[2,256,256]{2,1,0:T(8,128)(2,1)S(1)} all-to-all(bf16[2,256,256]{2,1,0:T(8,128)(2,1)S(1)} %broadcast_in_dim.23), channel_id=1, replica_groups=mesh['sub'=256,'sep'=2] {'sep'}, dimensions={0} | all-to-all | bytes 524288 | tf_op jit(solution)/shard_map/all_to_all | solution.py:25
  132.0 0.3 convolution_convert_fusion.2
  132.4 0.5 convolution_convert_fusion.5
  132.9 0.3 convolution_convert_fusion.6
  133.2 0.3 fusion.13
  133.6 0.7 fusion.51
  134.3 1.9 %gather_fusion = bf16[512,256]{1,0:T(8,128)(2,1)S(1)} fusion(bf16[480,256]{1,0:T(8,128)(2,1)S(1)} %get-tuple-element.53, s32[1024]{0:T(1024)S(1)} %pad_clamp_fusion), kind=kCustom, calls=%fused_computation | custom fusion | bytes 526336 | tf_op jit(solution)/shard_map/jit(_take)/gather | solution.py:138
  136.3 2.1 %fusion.1 = bf16[1,1,768,256]{2,3,1,0:T(8,128)(2,1)S(1)} fusion(f32[256,768]{1,0:T(8,128)S(1)} %copy-done.1, bf16[1,1,768,768]{3,2,1,0:T(8,128)(2,1)S(1)} %copy-done, bf16[1,1,512,768]{3,2,1,0:T(8,128)(2,1)} %param.21, bf16[512,256]{1,0:T(8,128)(2,1)S(1)} %gather_fusion, pred[512]{0:T(512)(128)(4,1)S(1)} %copy-done.23), kind=kOutput, calls=%fused_computation.5 | convolution fusion | flops 504037376 | bytes 3408384 | tf_op jit(solution)/shard_map/dot_general | solution.py:142
  138.4 0.9 copy.27
  (82 shorter events, 1.5 us)
Async XLA Ops:
  0.6 1.3 copy-start
  0.6 2.8 %copy-start.22 = (s32[1,1,512]{2,1,0:T(1,128)S(1)}, s32[1,1,512]{2,1,0:T(1,128)}, u32[]{:S(2)}) copy-start(s32[1,1,512]{2,1,0:T(1,128)} %param.22) | copy-start | bytes 6148
  0.7 2.8 %copy-start.4 = (bf16[1,1,512,768]{3,2,1,0:T(8,128)(2,1)S(1)}, bf16[1,1,512,768]{3,2,1,0:T(8,128)(2,1)}, u32[]{:S(2)}) copy-start(bf16[1,1,512,768]{3,2,1,0:T(8,128)(2,1)} %param.21) | copy-start | bytes 2359300
  3.4 5.5 %copy-start.20 = (bf16[1,32,64]{2,1,0:T(8,128)(2,1)S(1)}, bf16[1,32,64]{2,1,0:T(8,128)(2,1)}, u32[]{:S(2)}) copy-start(bf16[1,32,64]{2,1,0:T(8,128)(2,1)} %param.23) | copy-start | bytes 12292
  3.4 6.5 %copy-start.2 = (bf16[1,256,512]{2,1,0:T(8,128)(2,1)S(1)}, bf16[1,256,512]{2,1,0:T(8,128)(2,1)}, u32[]{:S(2)}) copy-start(bf16[1,256,512]{2,1,0:T(8,128)(2,1)} %param.26) | copy-start | bytes 786436
  3.4 6.6 %copy-start.17 = (bf16[1,64,128]{2,1,0:T(8,128)(2,1)S(1)}, bf16[1,64,128]{2,1,0:T(8,128)(2,1)}, u32[]{:S(2)}) copy-start(bf16[1,64,128]{2,1,0:T(8,128)(2,1)} %param.24) | copy-start | bytes 49156
  4.8 15.3 %copy-start.19 = (bf16[1,64,64]{2,1,0:T(8,128)(2,1)S(1)}, bf16[1,64,64]{2,1,0:T(8,128)(2,1)}, u32[]{:S(2)}) copy-start(bf16[1,64,64]{2,1,0:T(8,128)(2,1)} %param.27) | copy-start | bytes 24580
  4.8 7.9 %collective-permute-start = (bf16[480,256]{1,0:T(8,128)(2,1)}, bf16[480,256]{1,0:T(8,128)(2,1)S(1)}, u32[]{:S(2)}, u32[]{:S(2)}) collective-permute-start(bf16[480,256]{1,0:T(8,128)(2,1)} %get-tuple-element.54), channel_id=1, source_target_pairs={{0,2},{2,0},{4,6},{6,4},{8,10},{10,8},{12,14},{14,12},{16,18},{18,... | collective-permute-start | bytes 737288 | tf_op jit(solution)/shard_map/ppermute | solution.py:39
  9.0 11.2 %copy-start.7 = (bf16[1,256,256]{2,1,0:T(8,128)(2,1)S(1)}, bf16[1,256,256]{2,1,0:T(8,128)(2,1)}, u32[]{:S(2)}) copy-start(bf16[1,256,256]{2,1,0:T(8,128)(2,1)} %param.29) | copy-start | bytes 393220
  13.4 10.5 %collective-permute-start.1 = (bf16[480,256]{1,0:T(8,128)(2,1)}, bf16[480,256]{1,0:T(8,128)(2,1)S(1)}, u32[]{:S(2)}, u32[]{:S(2)}) collective-permute-start(bf16[480,256]{1,0:T(8,128)(2,1)} %fusion.21), channel_id=1, source_target_pairs={{0,4},{4,0},{2,6},{6,2},{8,12},{12,8},{10,14},{14,10},{16,20},{20,... | collective-permute-start | bytes 737288 | tf_op jit(solution)/shard_map/ppermute | solution.py:39
  23.9 14.3 %copy-start.16 = (bf16[1,128,128]{2,1,0:T(8,128)(2,1)S(1)}, bf16[1,128,128]{2,1,0:T(8,128)(2,1)}, u32[]{:S(2)}) copy-start(bf16[1,128,128]{2,1,0:T(8,128)(2,1)} %param.28) | copy-start | bytes 98308
  36.1 24.2 %copy-start.12 = (bf16[2,32,256]{2,1,0:T(8,128)(2,1)}, bf16[2,32,256]{2,1,0:T(8,128)(2,1)S(1)}, u32[]{:S(2)}) copy-start(bf16[2,32,256]{2,1,0:T(8,128)(2,1)S(1)} %all_to_all.23) | copy-start | bytes 98308
  36.3 8.7 %collective-permute-start.2 = (bf16[448,256]{1,0:T(8,128)(2,1)S(1)}, bf16[448,256]{1,0:T(8,128)(2,1)S(1)}, u32[]{:S(2)}, u32[]{:S(2)}) collective-permute-start(bf16[448,256]{1,0:T(8,128)(2,1)S(1)} %convert_element_type.135), channel_id=1, source_target_pairs={{0,8},{8,0},{2,10},{10,2},{4,12},{12,4},{6,14},{14,6},{16,24},{24,... | collective-permute-start | bytes 688136 | tf_op jit(solution)/shard_map/ppermute | solution.py:39
  45.0 15.2 %collective-permute-start.3 = (bf16[448,256]{1,0:T(8,128)(2,1)S(1)}, bf16[448,256]{1,0:T(8,128)(2,1)S(1)}, u32[]{:S(2)}, u32[]{:S(2)}) collective-permute-start(bf16[448,256]{1,0:T(8,128)(2,1)S(1)} %fusion.22), channel_id=1, source_target_pairs={{0,16},{16,0},{2,18},{18,2},{4,20},{20,4},{6,22},{22,6},{8,24},{24... | collective-permute-start | bytes 688136 | tf_op jit(solution)/shard_map/ppermute | solution.py:39
  66.3 0.6 copy-start.5
  67.0 16.1 %collective-permute-start.4 = (bf16[384,256]{1,0:T(8,128)(2,1)S(1)}, bf16[384,256]{1,0:T(8,128)(2,1)S(1)}, u32[]{:S(2)}, u32[]{:S(2)}) collective-permute-start(bf16[384,256]{1,0:T(8,128)(2,1)S(1)} %convert_element_type.142), channel_id=1, source_target_pairs={{0,32},{32,0},{2,34},{34,2},{4,36},{36,4},{6,38},{38,6},{8,40},{40... | collective-permute-start | bytes 589832 | tf_op jit(solution)/shard_map/ppermute | solution.py:39
  83.1 11.0 %copy-start.15 = (bf16[1,128,256]{2,1,0:T(8,128)(2,1)S(1)}, bf16[1,128,256]{2,1,0:T(8,128)(2,1)}, u32[]{:S(2)}) copy-start(bf16[1,128,256]{2,1,0:T(8,128)(2,1)} %param.25) | copy-start | bytes 196612
  83.1 8.0 %collective-permute-start.5 = (bf16[384,256]{1,0:T(8,128)(2,1)S(1)}, bf16[384,256]{1,0:T(8,128)(2,1)S(1)}, u32[]{:S(2)}, u32[]{:S(2)}) collective-permute-start(bf16[384,256]{1,0:T(8,128)(2,1)S(1)} %fusion.23), channel_id=1, source_target_pairs={{0,64},{64,0},{2,66},{66,2},{4,68},{68,4},{6,70},{70,6},{8,72},{72... | collective-permute-start | bytes 589832 | tf_op jit(solution)/shard_map/ppermute | solution.py:39
  98.3 17.7 %copy-start.8 = (bf16[2,128,256]{2,1,0:T(8,128)(2,1)}, bf16[2,128,256]{2,1,0:T(8,128)(2,1)S(1)}, u32[]{:S(2)}) copy-start(bf16[2,128,256]{2,1,0:T(8,128)(2,1)S(1)} %all_to_all.25) | copy-start | bytes 393220
  98.5 10.8 %collective-permute-start.6 = (bf16[256,256]{1,0:T(8,128)(2,1)S(1)}, bf16[256,256]{1,0:T(8,128)(2,1)S(1)}, u32[]{:S(2)}, u32[]{:S(2)}) collective-permute-start(bf16[256,256]{1,0:T(8,128)(2,1)S(1)} %get-tuple-element.56), channel_id=1, source_target_pairs={{0,128},{128,0},{2,130},{130,2},{4,132},{132,4},{6,134},{134,6},{8... | collective-permute-start | bytes 393224 | tf_op jit(solution)/shard_map/ppermute | solution.py:39
  109.3 6.7 %copy-start.10 = (bf16[256,256]{1,0:T(8,128)(2,1)}, bf16[256,256]{1,0:T(8,128)(2,1)S(1)}, u32[]{:S(2)}) copy-start(bf16[256,256]{1,0:T(8,128)(2,1)S(1)} %collective-permute-done.6) | copy-start | bytes 393220
  110.0 13.5 %collective-permute-start.7 = (bf16[256,256]{1,0:T(8,128)(2,1)}, bf16[256,256]{1,0:T(8,128)(2,1)}, u32[]{:S(2)}, u32[]{:S(2)}) collective-permute-start(bf16[256,256]{1,0:T(8,128)(2,1)} %fusion.30), channel_id=1, source_target_pairs={{0,256},{256,0},{2,258},{258,2},{4,260},{260,4},{6,262},{262,6},{8... | collective-permute-start | bytes 393224 | tf_op jit(solution)/shard_map/ppermute | solution.py:39
  120.1 0.9 copy-start.11
  120.1 1.0 copy-start.14
  120.1 1.1 copy-start.18
  120.1 1.2 copy-start.21
  120.5 6.9 %copy-start.3 = (bf16[1,256,512]{2,1,0:T(8,128)(2,1)S(1)}, bf16[1,256,512]{2,1,0:T(8,128)(2,1)}, u32[]{:S(2)}) copy-start(bf16[1,256,512]{2,1,0:T(8,128)(2,1)} %param.26) | copy-start | bytes 786436
  127.8 4.5 %copy-start.9 = (bf16[2,128,256]{2,1,0:T(8,128)(2,1)S(1)}, bf16[2,128,256]{2,1,0:T(8,128)(2,1)}, u32[]{:S(2)}) copy-start(bf16[2,128,256]{2,1,0:T(8,128)(2,1)} %copy-done.8) | copy-start | bytes 393220
  132.0 0.9 copy-start.6
  132.3 0.9 copy-start.13
  134.3 2.0 %copy-start.1 = (f32[256,768]{1,0:T(8,128)S(1)}, f32[256,768]{1,0:T(8,128)}, u32[]{:S(2)}) copy-start(f32[256,768]{1,0:T(8,128)} %fusion.3) | copy-start | bytes 2359300
  134.3 2.0 %copy-start.23 = (pred[512]{0:T(512)(128)(4,1)S(1)}, pred[512]{0:T(512)(128)(4,1)}, u32[]{:S(2)}) copy-start(pred[512]{0:T(512)(128)(4,1)} %compare_and_fusion) | copy-start | bytes 1540
where the time goes:
time: 140 us; the launch traced here: 139 us
  waiting for transfers between devices  49.2 us (35%)
  blocking collectives  34.2 us (24%)
  starting transfers between devices  29.2 us (21%)
  local copies, waits for them, and re-layouts  11.1 us (8%)
  matrix products  9.02 us (6%)
  other arithmetic  5.31 us (4%)
    ppermute x8, waiting for transfers between devices, swapped(): return lax.ppermute(block, axis, route)  49.2 us
    ppermute x8, starting transfers between devices, swapped(): return lax.ppermute(block, axis, route)  29.2 us
    all_gather x4, blocking collectives, local(): lax.all_gather(rhs_half, 'sep', axis=0, tiled=True)  16.1 us
    all_to_all x4, blocking collectives, copy_for_each(): lax.all_to_all(jnp.broadcast_to(x[None], (devices, *x.shape)), axis, 0, 0...  15.5 us
    unnamed x58, local copies, waits for them, and re-layouts  4.15 us
    slice x7, local copies, waits for them, and re-layouts, gather_together(): tiles = lines[:, at:at + a.size].reshape(-1, *a.shape)  3.21 us
  transfers between devices with their start and end apart: 8, of which 8 were waited for; matrix products, arithmetic and copies ran while one was open for 6% of the time, Pallas kernels for 0%

commit v1 on v0

v1 whole, which is shorter than its diff:
```python
import functools

import jax
import jax.numpy as jnp
from jax import lax
from jax.experimental import pallas as pl
from jax.experimental.pallas import tpu as pltpu
from jax.sharding import PartitionSpec as P

MESH = pl.DeviceIdType.MESH
F32 = jnp.float32
BF16 = jnp.bfloat16
X, Y, Z, C = 4, 8, 8, 2
INNER, BOUND, SHOTS = 768, 512, 256
OWN = SHOTS // (X * C)
WIDE = 512


def mm(a, b):
    return lax.dot_general(a, b, (((1,), (0,)), ((), ())), preferred_element_type=F32)


def mm_nt(a, b):
    return lax.dot_general(a, b, (((1,), (1,)), ((), ())), preferred_element_type=F32)


def mm_tn(a, b):
    return lax.dot_general(a, b, (((0,), (0,)), ((), ())), preferred_element_type=F32)


def slots(shape, dim):
    at = lax.broadcasted_iota(jnp.int32, shape, dim)
    low = jnp.where(at < 448, at - 352, jnp.where(at < 480, at - 448, -1))
    return jnp.where(at < 256, at + 224, jnp.where(at < 384, at - 160, low))


def kernel(
    src_h, a_h, c_h, map_ref, s0_h, s1_h, s2_h, s3_h, k0_h, k1_h, k2_h,
    inner_ref, sep_ref,
    src, a, cm, s0, s1, s2, s3, k0, k1, k2,
    ih, lt, p1, w, xb, yb, e1, e2, g1, g2, g3, nn, direct,
    v3, v2, v1, b3, b2, b1, t3, t2, h3, h2, r3, r2, ob, dt,
    load_sem, fac_s, fac_r, p1_s, p1_r, p2_s, p2_r, p3_s, p3_r, p4_s, p4_r, p5_s, p5_r,
):
    sub = lax.axis_index("sub")
    core = lax.axis_index("sep")
    x = lax.rem(sub, X)
    y = lax.rem(sub // X, Y)
    z = sub // (X * Y)
    q = lax.rem(y, 4)
    quad = y - q
    own = x * C + core

    def at(xx, yy, zz, cc):
        return {"sub": zz * (X * Y) + yy * X + xx, "sep": cc}

    def x_peer(dx, dc):
        return lax.rem(x + dx, X), lax.rem(core + dc, C)

    def y_peer(j):
        return lax.rem(y + j, Y)

    def q_peer(j):
        return quad + lax.rem(q + j, 4)

    def z_peer(j):
        return lax.rem(z + j, Z)

    y_far = lax.rem(y + 4, Y)
    z_near = z + 1 - 2 * lax.rem(z, 2)
    lines = [(2, 0), (2, 1), (1, 0), (3, 0), (1, 1), (3, 1), (0, 1)]
    ring = [4, 3, 5, 2, 6, 1, 7]

    loads = [
        pltpu.make_async_copy(src_h, src, load_sem.at[0]),
        pltpu.make_async_copy(a_h, a, load_sem.at[1]),
        pltpu.make_async_copy(c_h, cm, load_sem.at[2]),
    ]
    facs = [(s0_h, s0), (s1_h, s1), (s2_h, s2), (s3_h, s3), (k0_h, k0), (k1_h, k1), (k2_h, k2)]
    for i, (h, v) in enumerate(facs):
        loads.append(pltpu.make_async_copy(h, v.at[core], load_sem.at[3 + i]))
    for copy in loads:
        copy.start()

    barrier = pltpu.get_barrier_semaphore()
    peers = [at(x_peer(dx, dc)[0], y, z, x_peer(dx, dc)[1]) for dx, dc in lines]
    peers += [at(x, y_peer(j), z, core) for j in ring]
    peers += [at(x, y, z_peer(j), core) for j in ring]
    peers += [at(x, y_far, z_near, core)]
    for peer in peers:
        pl.semaphore_signal(barrier, inc=1, device_id=peer, device_id_type=MESH)

    def send(source, target, s, r, peer):
        return pltpu.make_async_remote_copy(
            src_ref=source, dst_ref=target, send_sem=s, recv_sem=r, device_id=peer, device_id_type=MESH
        )

    onehot = (slots((WIDE, BOUND), 0) == map_ref[...]).astype(BF16)
    loads[0].wait()
    loads[1].wait()
    for i in range(3):
        lo, hi = 256 * i, 256 * (i + 1)
        ih[lo:hi, :] = mm(a[lo:hi, :hi], src[:hi, :]).astype(BF16)

    pl.semaphore_wait(barrier, len(peers))
    fac_copies = [
        send(h, v.at[core], fac_s.at[i], fac_r.at[i], at(x, y, z, 1 - core)) for i, (h, v) in enumerate(facs)
    ]
    for copy in fac_copies:
        copy.start()

    loads[2].wait()
    bh = mm(cm[...], ih[...])
    bht = bh.T.astype(BF16)
    lt[...] = mm_nt(bht, onehot).astype(BF16).reshape(X * C, OWN, WIDE)

    one = []
    for j, (dx, dc) in enumerate(lines):
        xx, cc = x_peer(dx, dc)
        one.append(send(lt.at[xx * C + cc], p1.at[own], p1_s.at[j], p1_r.at[j], at(xx, y, z, cc)))
    for copy in one:
        copy.start()
    p1[own] = lt[own]

    for copy in loads[3:]:
        copy.wait()
    for copy in fac_copies:
        copy.wait_recv()
    f0 = s0[...].reshape(64, 64)
    f1 = s1[...].reshape(128, 128)
    f2 = s2[...].reshape(256, 256)
    f3 = s3[...].reshape(512, 512)
    m0 = k0[...].reshape(128, 64)
    m1 = k1[...].reshape(256, 128)
    m2 = k2[...].reshape(512, 256)
    e0 = mm(m0, f0)
    e0t = e0.T.astype(BF16)
    e1[...] = mm(m1, f1).astype(BF16)
    e2[...] = mm(m2, f2).astype(BF16)
    g0 = mm_tn(f0, f0).astype(BF16)
    g1[...] = mm_tn(f1, f1).astype(BF16)
    g2[...] = mm_tn(f2, f2).astype(BF16)
    row = lax.broadcasted_iota(jnp.int32, (64, 128), 0)
    col = lax.broadcasted_iota(jnp.int32, (64, 128), 1)
    w[...] = jnp.zeros_like(w)
    yb[...] = jnp.zeros_like(yb)
    for p in range(2):
        w[128 * p : 128 * p + 64, :] = (col == row + 64 * p).astype(BF16)
        w[128 * p + 64 : 128 * p + 96, :] = e0t[32 * p : 32 * p + 32, :]
        part = jnp.concatenate([g0[32 * p : 32 * p + 32, 0:32], jnp.zeros((32, 32), BF16)], axis=1)
        other = jnp.concatenate([g0[32 * p : 32 * p + 32, 32:64], jnp.zeros((32, 32), BF16)], axis=1)
        blank = jnp.zeros((32, 64), BF16)
        yb[128 * p + 64 : 128 * p + 96, :] = jnp.concatenate([blank, part, blank, other], axis=1)
    wt = w[...].astype(F32).T
    lane = lax.rem(lax.broadcasted_iota(jnp.int32, (128, 256), 1), 128)
    xb[...] = jnp.where(lane < 64, wt, -wt).astype(BF16)

    for copy in one:
        copy.wait_recv()
    strips = []
    for p in range(2):
        total = p1[p].astype(F32)
        for xx in range(1, X):
            total = total + p1[xx * C + p].astype(F32)
        strips.append(total)
    tails = jnp.concatenate([strips[0][:, 384:], strips[1][:, 384:]], axis=1).astype(BF16)
    x1 = mm(tails, w[...])
    x1h = x1.astype(BF16)
    x2 = jnp.concatenate([strips[0][:, 256:384], strips[1][:, 256:384]], axis=1) + mm_nt(x1h, e1[...])
    x2h = x2.astype(BF16)
    x3 = jnp.concatenate([strips[0][:, :256], strips[1][:, :256]], axis=1) + mm_nt(x2h, e2[...])
    x3h = x3.astype(BF16)
    for k in range(8):
        v3[k] = x3h[16 * (k // 4) : 16 * (k // 4) + 16, 128 * (k % 4) : 128 * (k % 4) + 128]
    for k in range(4):
        v2[k] = x2h[16 * (k // 2) : 16 * (k // 2) + 16, 128 * (k % 2) : 128 * (k % 2) + 128]
    v1[...] = x1h

    two = []
    for j in ring:
        yy = y_peer(j)
        two.append(send(v3.at[yy], b3.at[j], p2_s.at[j], p2_r.at[j], at(x, yy, z, core)))
    for j in range(1, 4):
        yy = q_peer(j)
        two.append(send(v2.at[yy - quad], b2.at[j], p2_s.at[8 + j], p2_r.at[8 + j], at(x, yy, z, core)))
    for j in range(1, 4):
        two.append(send(v1, b1.at[j], p2_s.at[12 + j], p2_r.at[12 + j], at(x, q_peer(j), z, core)))
    for copy in two:
        copy.start()

    g3[...] = mm_tn(f3, f3).astype(BF16)

    for copy in two[:7]:
        copy.wait_recv()
    sum3 = v3[y].astype(F32)
    for j in range(1, 8):
        sum3 = sum3 + b3[j].astype(F32)
    t3[...] = sum3.astype(BF16)
    three = []
    for j in ring:
        three.append(send(t3, h3.at[j], p3_s.at[j], p3_r.at[j], at(x, y, z_peer(j), core)))
    for copy in three:
        copy.start()
    for copy in two[7:10]:
        copy.wait_recv()
    sum2 = v2[q].astype(F32)
    for j in range(1, 4):
        sum2 = sum2 + b2[j].astype(F32)
    t2[...] = sum2.astype(BF16)
    far = [(y_far, z), (y, z_near), (y_far, z_near)]
    for j, (yy, zz) in enumerate(far):
        three.append(send(t2, h2.at[j], p3_s.at[8 + j], p3_r.at[8 + j], at(x, yy, zz, core)))
        three[-1].start()

    for i in range(3):
        lo, hi = 256 * i, 256 * (i + 1)
        direct[lo:hi, :] = mm_tn(a[lo:, lo:hi], ih[lo:, :])
    picked_rows = mm(onehot, cm[...]).astype(BF16)
    for i in range(3):
        lo, hi = 256 * i, 256 * (i + 1)
        nn[lo:hi, :] = mm(picked_rows[:, lo:], a[lo:, lo:hi]).T.astype(BF16)
    out_slot = lax.broadcasted_iota(jnp.int32, (480, WIDE), 0)
    nn[INNER:, :] = (slots((480, WIDE), 1) == out_slot).astype(BF16)

    for copy in three[:7]:
        copy.wait_recv()
    top = t3[...].astype(F32)
    for j in range(1, 8):
        top = top + h3[j].astype(F32)
    r3[y] = top.astype(BF16)
    four = []
    for j in ring:
        four.append(send(r3.at[y], r3.at[y], p4_s.at[j], p4_r.at[j], at(x, y_peer(j), z, core)))
    for copy in four:
        copy.start()
    for copy in three[7:]:
        copy.wait_recv()
    mid = t2[...].astype(F32)
    for j in range(3):
        mid = mid + h2[j].astype(F32)
    r2[q] = mid.astype(BF16)
    for j in range(1, 4):
        four.append(send(r2.at[q], r2.at[q], p4_s.at[8 + j], p4_r.at[8 + j], at(x, q_peer(j), z, core)))
        four[-1].start()

    for copy in two[10:]:
        copy.wait_recv()
    low = v1[...].astype(F32)
    for j in range(1, 4):
        low = low + b1[j].astype(F32)
    own1 = mm(low.astype(BF16), g1[...])
    own0 = mm(tails, yb[...])
    for copy in four[7:]:
        copy.wait_recv()
    whole2 = jnp.concatenate(
        [jnp.concatenate([r2[2 * i], r2[2 * i + 1]], axis=1) for i in range(2)], axis=0
    )
    own2 = mm(whole2, g2[...])
    for copy in four[:7]:
        copy.wait_recv()
    whole3 = jnp.concatenate(
        [jnp.concatenate([r3[4 * i + k] for k in range(4)], axis=1) for i in range(2)], axis=0
    )
    d3 = mm(whole3, g3[...]).astype(BF16)
    d2 = (own2 - mm(d3, e2[...])).astype(BF16)
    d1 = (own1 - mm(d2, e1[...])).astype(BF16)
    d0 = (own0 + mm(d1, xb[...])).astype(BF16)
    for p in range(2):
        ob[p] = jnp.concatenate(
            [d3[:, 256 * p : 256 * p + 256], d2[:, 128 * p : 128 * p + 128], d0[:, 128 * p : 128 * p + 128]], axis=1
        )

    five = []
    for j, (dx, dc) in enumerate(lines):
        xx, cc = x_peer(dx, dc)
        five.append(send(ob.at[cc], dt.at[own], p5_s.at[j], p5_r.at[j], at(xx, y, z, cc)))
    for copy in five:
        copy.start()
    dt[own] = ob[core]
    for copy in five:
        copy.wait_recv()
    down = dt[...].reshape(SHOTS, WIDE)
    for i in range(3):
        lo, hi = 256 * i, 256 * (i + 1)
        inner_ref[lo:hi, :] = (direct[lo:hi, :] - mm_nt(nn[lo:hi, :], down)).astype(BF16)
    sep_ref[...] = mm_nt(nn[INNER:, :], down).astype(BF16)
    for copy in fac_copies + one + two + three + four + five:
        copy.wait_send()


def local(
    sources, inner_inv, coupling, boundary_map,
    sep_inv_0, sep_inv_1, sep_inv_2, sep_inv_3, sep_couple_0, sep_couple_1, sep_couple_2,
):
    hbm = pl.BlockSpec(memory_space=pl.ANY)
    vmem = pl.BlockSpec(memory_space=pltpu.VMEM)
    v = pltpu.VMEM
    dma = pltpu.SemaphoreType.DMA
    scratch = [
        v((INNER, SHOTS), BF16), v((INNER, INNER), BF16), v((BOUND, INNER), BF16),
        v((2, 32, 64), BF16), v((2, 64, 128), BF16), v((2, 128, 256), BF16), v((2, 256, 512), BF16),
        v((2, 64, 64), BF16), v((2, 128, 128), BF16), v((2, 256, 256), BF16),
        v((INNER, SHOTS), BF16), v((X * C, OWN, WIDE), BF16), v((X * C, OWN, WIDE), BF16),
        v((256, 128), BF16), v((128, 256), BF16), v((256, 256), BF16),
        v((256, 128), BF16), v((512, 256), BF16),
        v((128, 128), BF16), v((256, 256), BF16), v((512, 512), BF16),
        v((INNER + 480, WIDE), BF16), v((INNER, SHOTS), F32),
        v((8, 16, 128), BF16), v((4, 16, 128), BF16), v((32, 128), BF16),
        v((8, 16, 128), BF16), v((4, 16, 128), BF16), v((4, 32, 128), BF16),
        v((16, 128), BF16), v((16, 128), BF16), v((8, 16, 128), BF16), v((3, 16, 128), BF16),
        v((8, 16, 128), BF16), v((4, 16, 128), BF16),
        v((2, OWN, WIDE), BF16), v((X * C, OWN, WIDE), BF16),
        dma((10,)), dma((7,)), dma((7,)), dma((7,)), dma((7,)), dma((16,)), dma((16,)),
        dma((11,)), dma((11,)), dma((12,)), dma((12,)), dma((7,)), dma((7,)),
    ]
    inner, sep = pl.pallas_call(
        kernel,
        out_shape=(
            jax.ShapeDtypeStruct((INNER, SHOTS), BF16),
            jax.ShapeDtypeStruct((480, SHOTS), BF16),
        ),
        in_specs=[hbm, hbm, hbm, vmem] + [hbm] * 7,
        out_specs=(vmem, vmem),
        scratch_shapes=scratch,
        compiler_params=pltpu.CompilerParams(collective_id=0, has_side_effects=True),
    )(
        sources[0, 0], inner_inv[0, 0], coupling[0, 0], boundary_map[0],
        sep_inv_0[0], sep_inv_1[0], sep_inv_2[0], sep_inv_3[0],
        sep_couple_0[0], sep_couple_1[0], sep_couple_2[0],
    )
    return inner[None, None], sep[None, None]


def solution(mesh):
    leaf, factor = P("sub", "sep", None, None), P("sub", "sep", None)
    return jax.shard_map(
        local,
        mesh=mesh,
        in_specs=(leaf, leaf, leaf, factor) + (factor,) * 7,
        out_specs=(leaf, leaf),
        check_vma=False,
    )
```

time: 140 us -> 47.5 us (0.34)
  waiting for transfers between devices: 49.2 us -> 0 us
  Pallas kernels: 0 us -> 43.2 us
  blocking collectives: 34.2 us -> 0 us
  starting transfers between devices: 29.2 us -> 0 us
  matrix products: 9.02 us -> 0 us
  local copies, waits for them, and re-layouts: 11.1 us -> 3.42 us
  other arithmetic: 5.31 us -> 0 us
    ppermute x8 -> x0, waiting for transfers between devices: 49.2 us -> none  [swapped(): return lax.ppermute(block, axis, route)]
    pallas_call x0 -> x1, Pallas kernels: none -> 43.2 us  [local(): pl.pallas_call(kernel, out_shape=(jax.ShapeDtypeStruct((INNER, SHOTS), BF...]
    ppermute x8 -> x0, starting transfers between devices: 29.2 us -> none  [swapped(): return lax.ppermute(block, axis, route)]
    all_gather x5 -> x0, blocking collectives: 18.7 us -> none  [the longest x4 16.1 us: local(): lax.all_gather(rhs_half, 'sep', axis=0, tiled=True)]
    all_to_all x4 -> x0, blocking collectives: 15.5 us -> none  [copy_for_each(): lax.all_to_all(jnp.broadcast_to(x[None], (devices, *x.shape)), axis, 0, 0...]
    dot_general x15 -> x0, matrix products: 9.02 us -> none  [the longest x1 2.1 us: local(): lax.dot_general(inverse, lifted, (((0,), (0,)), ((), ())), preferred_elem...]
    slice x12 -> x0, local copies, waits for them, and re-layouts: 3.29 us -> none  [the longest x7 3.21 us: gather_together(): tiles = lines[:, at:at + a.size].reshape(-1, *a.shape)]
    convert_element_type x7 -> x0, other arithmetic: 2.6 us -> none  [the longest x6 1.59 us: local(): carried.astype(jnp.bfloat16)]
  transfers between devices with their start and end apart: 8 -> 0, of which waited for: 8 -> 0; matrix products, arithmetic and copies ran while one was open for 6% -> 0% of each run, Pallas kernels for 0% -> 0%
where the time goes in v1:
time: 47.5 us; the launch traced here: 47.3 us
  Pallas kernels  43.2 us (91%)
  local copies, waits for them, and re-layouts  3.42 us (7%)
  between operations  0.64 us (1%)
    pallas_call x1, Pallas kernels, local(): pl.pallas_call(kernel, out_shape=(jax.ShapeDtypeStruct((INNER, SHOTS), BF...  43.2 us
    unnamed x2, local copies, waits for them, and re-layouts  3.42 us

profile of v1, /device:TPU:1, one launch (start us, length us, event | category | flops | bytes accessed | tf_op | source)
XLA Modules:
  0.0 47.3 jit_solution(17836183623098009169)
XLA Ops:
  0.6 43.2 %shard_map.122 = (bf16[768,256]{1,0:T(8,128)(2,1)}, bf16[480,256]{1,0:T(8,128)(2,1)}) custom-call(bf16[768,256]{1,0:T(8,128)(2,1)} %bitcast.15, bf16[768,768]{1,0:T(8,128)(2,1)} %bitcast.13, bf16[512,768]{1,0:T(8,128)(2,1)} %bitcast.14, s32[1,512]{1,0:T(1,128)} %bitcast.25, bf16[32,64]{1,0:T(8,128)(2,1)} %bitcast.24, bf16[64,128]{1,0:T(8,128)(2,1)} %bitcast.22, ...), custom_call_target="tpu_custom_call" | custom-call | tf_op jit(solution)/shard_map/pallas_call | solution.py:316
  43.9 1.8 %copy.15 = bf16[1,1,768,256]{3,2,1,0:T(8,128)(2,1)} copy(bf16[1,1,768,256]{3,2,1,0:T(8,128)(2,1)} %bitcast.16) | data formatting | bytes 786432
  45.7 1.7 %copy.16 = bf16[1,1,480,256]{3,2,1,0:T(8,128)(2,1)} copy(bf16[1,1,480,256]{3,2,1,0:T(8,128)(2,1)} %bitcast.18) | data formatting | bytes 491520

commit v2 on v1

v2 whole, which is shorter than its diff:
```python
import functools

import jax
import jax.numpy as jnp
from jax import lax
from jax.experimental import pallas as pl
from jax.experimental.pallas import tpu as pltpu
from jax.sharding import PartitionSpec as P

MESH = pl.DeviceIdType.MESH
F32 = jnp.float32
BF16 = jnp.bfloat16
X, Y, Z, C = 4, 8, 8, 2
INNER, BOUND, SHOTS = 768, 512, 256
OWN = SHOTS // (X * C)
WIDE = 512


def mm(a, b):
    return lax.dot_general(a, b, (((1,), (0,)), ((), ())), preferred_element_type=F32)


def mm_nt(a, b):
    return lax.dot_general(a, b, (((1,), (1,)), ((), ())), preferred_element_type=F32)


def mm_tn(a, b):
    return lax.dot_general(a, b, (((0,), (0,)), ((), ())), preferred_element_type=F32)


def slots(shape, dim):
    at = lax.broadcasted_iota(jnp.int32, shape, dim)
    low = jnp.where(at < 448, at - 352, jnp.where(at < 480, at - 448, -1))
    return jnp.where(at < 256, at + 224, jnp.where(at < 384, at - 160, low))


def kernel(
    src_h, a_h, c_h, map_h, s0_h, s1_h, s2_h, s3_h, k0_h, k1_h, k2_h,
    inner_ref, sep_ref,
    src, a, cm, mp, s0, s1, s2, s3, k0, k1, k2,
    ih, lt3, ltr, p3, pr, w, xb, yb, e1, e2, g1, g2, g3, nn, direct,
    v3, v2, v1, b3, b2, b1, t3, t2, h3, h2, r3, r2, o3, orr, d3a, dra,
    load_sem, fac_s, fac_r, p1_s, p1_r, p2_s, p2_r, p3_s, p3_r, p4_s, p4_r, p5_s, p5_r,
):
    sub = lax.axis_index("sub")
    core = lax.axis_index("sep")
    x = lax.rem(sub, X)
    y = lax.rem(sub // X, Y)
    z = sub // (X * Y)
    q = lax.rem(y, 4)
    quad = y - q
    own = x * C + core

    def at(xx, yy, zz, cc):
        return {"sub": zz * (X * Y) + yy * X + xx, "sep": cc}

    def x_peer(dx, dc):
        return lax.rem(x + dx, X), lax.rem(core + dc, C)

    def y_peer(j):
        return lax.rem(y + j, Y)

    def q_peer(j):
        return quad + lax.rem(q + j, 4)

    def z_peer(j):
        return lax.rem(z + j, Z)

    z_near = z + 1 - 2 * lax.rem(z, 2)
    lines = [(2, 0), (2, 1), (1, 0), (3, 0), (1, 1), (3, 1), (0, 1)]
    ring = [4, 3, 5, 2, 6, 1, 7]

    barrier = pltpu.get_barrier_semaphore()
    peers = [at(x, y, z_peer(j), core) for j in ring]
    peers += [at(x, y_peer(j), z, core) for j in ring]
    peers += [at(x_peer(dx, dc)[0], y, z, x_peer(dx, dc)[1]) for dx, dc in lines]
    for peer in peers:
        pl.semaphore_signal(barrier, inc=1, device_id=peer, device_id_type=MESH)

    loads = [pltpu.make_async_copy(map_h, mp, load_sem.at[0])]
    loads.append(pltpu.make_async_copy(src_h, src, load_sem.at[1]))
    for i in range(3):
        lo, hi = 256 * i, 256 * (i + 1)
        loads.append(pltpu.make_async_copy(a_h.at[lo:hi, :hi], a.at[lo:hi, :hi], load_sem.at[2 + i]))
    loads.append(pltpu.make_async_copy(c_h, cm, load_sem.at[5]))
    facs = [(s0_h, s0), (s1_h, s1), (s2_h, s2), (s3_h, s3), (k0_h, k0), (k1_h, k1), (k2_h, k2)]
    for i, (h, v) in enumerate(facs):
        loads.append(pltpu.make_async_copy(h, v.at[core], load_sem.at[6 + i]))
    for copy in loads:
        copy.start()

    def send(source, target, s, r, peer):
        return pltpu.make_async_remote_copy(
            src_ref=source, dst_ref=target, send_sem=s, recv_sem=r, device_id=peer, device_id_type=MESH
        )

    loads[0].wait()
    onehot = (slots((WIDE, BOUND), 0) == mp[...]).astype(BF16)
    loads[1].wait()
    for i in range(3):
        lo, hi = 256 * i, 256 * (i + 1)
        loads[2 + i].wait()
        ih[lo:hi, :] = mm(a[lo:hi, :hi], src[:hi, :]).astype(BF16)
    loads[5].wait()
    bh = mm(cm[...], ih[...])
    bht = bh.T.astype(BF16)
    ltr[...] = mm_nt(bht, onehot[256:, :]).astype(BF16).reshape(X * C, OWN, 256)
    pl.semaphore_wait(barrier, len(peers))

    one = []
    for half, (source, target) in enumerate([(ltr, pr), (lt3, p3)]):
        for j, (dx, dc) in enumerate(lines):
            xx, cc = x_peer(dx, dc)
            k = 7 * half + j
            one.append(send(source.at[xx * C + cc], target.at[own], p1_s.at[k], p1_r.at[k], at(xx, y, z, cc)))
    for copy in one[:7]:
        copy.start()
    lt3[...] = mm_nt(bht, onehot[:256, :]).astype(BF16).reshape(X * C, OWN, 256)
    for copy in one[7:]:
        copy.start()
    fac_copies = [
        send(h, v.at[core], fac_s.at[i], fac_r.at[i], at(x, y, z, 1 - core)) for i, (h, v) in enumerate(facs)
    ]
    for copy in fac_copies:
        copy.start()
    pr[own] = ltr[own]
    p3[own] = lt3[own]

    for copy in loads[6:]:
        copy.wait()
    for copy in fac_copies:
        copy.wait_recv()
    f0 = s0[...].reshape(64, 64)
    f1 = s1[...].reshape(128, 128)
    f2 = s2[...].reshape(256, 256)
    f3 = s3[...].reshape(512, 512)
    m0 = k0[...].reshape(128, 64)
    m1 = k1[...].reshape(256, 128)
    m2 = k2[...].reshape(512, 256)
    e0 = mm(m0, f0)
    e0t = e0.T.astype(BF16)
    e1[...] = mm(m1, f1).astype(BF16)
    e2[...] = mm(m2, f2).astype(BF16)
    w[...] = jnp.zeros_like(w)
    row = lax.broadcasted_iota(jnp.int32, (64, 128), 0)
    col = lax.broadcasted_iota(jnp.int32, (64, 128), 1)
    for p in range(2):
        w[128 * p : 128 * p + 64, :] = (col == row + 64 * p).astype(BF16)
        w[128 * p + 64 : 128 * p + 96, :] = e0t[32 * p : 32 * p + 32, :]

    def line_sum(buffer, p):
        total = buffer[p].astype(F32)
        for xx in range(1, X):
            total = total + buffer[xx * C + p].astype(F32)
        return total

    for copy in one[:7]:
        copy.wait_recv()
    rest = [line_sum(pr, p) for p in range(2)]
    tails = jnp.concatenate([rest[0][:, 128:], rest[1][:, 128:]], axis=1).astype(BF16)
    x1h = mm(tails, w[...]).astype(BF16)
    x2 = jnp.concatenate([rest[0][:, :128], rest[1][:, :128]], axis=1) + mm_nt(x1h, e1[...])
    x2h = x2.astype(BF16)
    x3 = mm_nt(x2h, e2[...])
    for k in range(4):
        v2[k] = x2h[16 * (k // 2) : 16 * (k // 2) + 16, 128 * (k % 2) : 128 * (k % 2) + 128]
    v1[...] = x1h
    for copy in one[7:]:
        copy.wait_recv()
    x3h = (x3 + jnp.concatenate([line_sum(p3, 0), line_sum(p3, 1)], axis=1)).astype(BF16)
    for k in range(8):
        v3[k] = x3h[16 * (k // 4) : 16 * (k // 4) + 16, 128 * (k % 4) : 128 * (k % 4) + 128]

    two = []
    for j in ring:
        yy = y_peer(j)
        two.append(send(v3.at[yy], b3.at[j], p2_s.at[j], p2_r.at[j], at(x, yy, z, core)))
    for j in ring:
        yy = y_peer(j)
        two.append(send(v2.at[lax.rem(yy, 4)], b2.at[j], p2_s.at[8 + j], p2_r.at[8 + j], at(x, yy, z, core)))
    for j in range(1, 4):
        two.append(send(v1, b1.at[j], p2_s.at[16 + j], p2_r.at[16 + j], at(x, q_peer(j), z, core)))
    for copy in two[:14]:
        copy.start()

    g0 = mm_tn(f0, f0).astype(BF16)
    g1[...] = mm_tn(f1, f1).astype(BF16)
    g2[...] = mm_tn(f2, f2).astype(BF16)
    g3[...] = mm_tn(f3, f3).astype(BF16)
    yb[...] = jnp.zeros_like(yb)
    blank = jnp.zeros((32, 64), BF16)
    gap = jnp.zeros((32, 32), BF16)
    for p in range(2):
        rows = g0[32 * p : 32 * p + 32, :]
        yb[128 * p + 64 : 128 * p + 96, :] = jnp.concatenate([blank, rows[:, :32], gap, blank, rows[:, 32:], gap], axis=1)
    wt = w[...].astype(F32).T
    lane = lax.rem(lax.broadcasted_iota(jnp.int32, (128, 256), 1), 128)
    xb[...] = jnp.where(lane < 64, wt, -wt).astype(BF16)

    for copy in two[:7]:
        copy.wait_recv()
    sum3 = v3[y].astype(F32)
    for j in range(1, 8):
        sum3 = sum3 + b3[j].astype(F32)
    t3[...] = sum3.astype(BF16)
    three = []
    for j in ring:
        three.append(send(t3, h3.at[j], p3_s.at[j], p3_r.at[j], at(x, y, z_peer(j), core)))
    for copy in three:
        copy.start()
    for copy in two[7:14]:
        copy.wait_recv()
    sum2 = v2[q].astype(F32)
    for j in range(1, 8):
        sum2 = sum2 + b2[j].astype(F32)
    t2[...] = sum2.astype(BF16)
    three.append(send(t2, h2, p3_s.at[8], p3_r.at[8], at(x, y, z_near, core)))
    three[-1].start()
    for copy in two[14:]:
        copy.start()

    for i in range(3):
        lo, hi = 256 * i, 256 * (i + 1)
        direct[lo:hi, :] = mm_tn(a[lo:, lo:hi], ih[lo:, :])
    picked_rows = mm(onehot, cm[...]).astype(BF16)
    for i in range(3):
        lo, hi = 256 * i, 256 * (i + 1)
        nn[lo:hi, :] = mm(picked_rows[:, lo:], a[lo:, lo:hi]).T.astype(BF16)
    out_slot = lax.broadcasted_iota(jnp.int32, (480, WIDE), 0)
    nn[INNER:, :] = (slots((480, WIDE), 1) == out_slot).astype(BF16)

    for copy in three[:7]:
        copy.wait_recv()
    top = t3[...].astype(F32)
    for j in range(1, 8):
        top = top + h3[j].astype(F32)
    r3[y] = top.astype(BF16)
    four = []
    for j in ring:
        four.append(send(r3.at[y], r3.at[y], p4_s.at[j], p4_r.at[j], at(x, y_peer(j), z, core)))
    for copy in four:
        copy.start()
    three[7].wait_recv()
    r2[q] = (t2[...].astype(F32) + h2[...].astype(F32)).astype(BF16)
    for j in range(1, 4):
        four.append(send(r2.at[q], r2.at[q], p4_s.at[8 + j], p4_r.at[8 + j], at(x, q_peer(j), z, core)))
        four[-1].start()

    for copy in two[14:]:
        copy.wait_recv()
    low = v1[...].astype(F32)
    for j in range(1, 4):
        low = low + b1[j].astype(F32)
    own1 = mm(low.astype(BF16), g1[...])
    own0 = mm(tails, yb[...])
    for copy in four[7:]:
        copy.wait_recv()
    whole2 = jnp.concatenate(
        [jnp.concatenate([r2[2 * i], r2[2 * i + 1]], axis=1) for i in range(2)], axis=0
    )
    own2 = mm(whole2, g2[...])
    for copy in four[:7]:
        copy.wait_recv()
    whole3 = jnp.concatenate(
        [jnp.concatenate([r3[4 * i + k] for k in range(4)], axis=1) for i in range(2)], axis=0
    )
    d3 = mm(whole3, g3[...]).astype(BF16)
    for p in range(2):
        o3[p] = d3[:, 256 * p : 256 * p + 256]

    five = []
    for half, (source, target) in enumerate([(o3, d3a), (orr, dra)]):
        for j, (dx, dc) in enumerate(lines):
            xx, cc = x_peer(dx, dc)
            k = 7 * half + j
            five.append(send(source.at[cc], target.at[own], p5_s.at[k], p5_r.at[k], at(xx, y, z, cc)))
    for copy in five[:7]:
        copy.start()
    d3a[own] = o3[core]
    d2 = (own2 - mm(d3, e2[...])).astype(BF16)
    d1 = (own1 - mm(d2, e1[...])).astype(BF16)
    d0 = (own0 + mm(d1, xb[...])).astype(BF16)
    for p in range(2):
        orr[p] = jnp.concatenate([d2[:, 128 * p : 128 * p + 128], d0[:, 128 * p : 128 * p + 128]], axis=1)
    for copy in five[7:]:
        copy.start()
    dra[own] = orr[core]
    for copy in five[:7]:
        copy.wait_recv()
    down3 = d3a[...].reshape(SHOTS, 256)
    for i in range(3):
        lo, hi = 256 * i, 256 * (i + 1)
        direct[lo:hi, :] = direct[lo:hi, :] - mm_nt(nn[lo:hi, :256], down3)
    sep_ref[224:, :] = mm_nt(nn[INNER + 224 :, :256], down3).astype(BF16)
    for copy in five[7:]:
        copy.wait_recv()
    downr = dra[...].reshape(SHOTS, 256)
    for i in range(3):
        lo, hi = 256 * i, 256 * (i + 1)
        inner_ref[lo:hi, :] = (direct[lo:hi, :] - mm_nt(nn[lo:hi, 256:], downr)).astype(BF16)
    sep_ref[:224, :] = mm_nt(nn[INNER : INNER + 224, 256:], downr).astype(BF16)
    for copy in fac_copies + one + two + three + four + five:
        copy.wait_send()


def write_out(inner, sep, inner_h, sep_h, sem):
    copies = [
        pltpu.make_async_copy(inner, inner_h, sem.at[0]),
        pltpu.make_async_copy(sep, sep_h, sem.at[1]),
    ]
    for copy in copies:
        copy.start()
    for copy in copies:
        copy.wait()


def local(
    sources, inner_inv, coupling, boundary_map,
    sep_inv_0, sep_inv_1, sep_inv_2, sep_inv_3, sep_couple_0, sep_couple_1, sep_couple_2,
):
    held = [
        sources[0, 0], inner_inv[0, 0], coupling[0, 0], boundary_map[0],
        sep_inv_0[0], sep_inv_1[0], sep_inv_2[0], sep_inv_3[0],
        sep_couple_0[0], sep_couple_1[0], sep_couple_2[0],
    ]
    held = [pltpu.with_memory_space_constraint(v, pltpu.HBM) for v in held]
    hbm = pl.BlockSpec(memory_space=pltpu.HBM)
    vmem = pl.BlockSpec(memory_space=pltpu.VMEM)
    v = pltpu.VMEM
    dma = pltpu.SemaphoreType.DMA
    piece = v((X * C, OWN, 256), BF16)
    scratch = [
        v((INNER, SHOTS), BF16), v((INNER, INNER), BF16), v((BOUND, INNER), BF16), v((1, BOUND), jnp.int32),
        v((2, 32, 64), BF16), v((2, 64, 128), BF16), v((2, 128, 256), BF16), v((2, 256, 512), BF16),
        v((2, 64, 64), BF16), v((2, 128, 128), BF16), v((2, 256, 256), BF16),
        v((INNER, SHOTS), BF16), piece, piece, piece, piece,
        v((256, 128), BF16), v((128, 256), BF16), v((256, 256), BF16),
        v((256, 128), BF16), v((512, 256), BF16),
        v((128, 128), BF16), v((256, 256), BF16), v((512, 512), BF16),
        v((INNER + 480, WIDE), BF16), v((INNER, SHOTS), F32),
        v((8, 16, 128), BF16), v((4, 16, 128), BF16), v((32, 128), BF16),
        v((8, 16, 128), BF16), v((8, 16, 128), BF16), v((4, 32, 128), BF16),
        v((16, 128), BF16), v((16, 128), BF16), v((8, 16, 128), BF16), v((16, 128), BF16),
        v((8, 16, 128), BF16), v((4, 16, 128), BF16),
        v((2, OWN, 256), BF16), v((2, OWN, 256), BF16), piece, piece,
        dma((13,)), dma((7,)), dma((7,)), dma((14,)), dma((14,)), dma((20,)), dma((20,)),
        dma((9,)), dma((9,)), dma((12,)), dma((12,)), dma((14,)), dma((14,)),
    ]
    inner, sep = pl.pallas_call(
        kernel,
        out_shape=(
            jax.ShapeDtypeStruct((INNER, SHOTS), BF16),
            jax.ShapeDtypeStruct((480, SHOTS), BF16),
        ),
        in_specs=[hbm] * 11,
        out_specs=(vmem, vmem),
        scratch_shapes=scratch,
        compiler_params=pltpu.CompilerParams(
            collective_id=0, has_side_effects=True, vmem_limit_bytes=24 * 1024 * 1024
        ),
    )(*held)
    inner, sep = pl.pallas_call(
        write_out,
        out_shape=(
            jax.ShapeDtypeStruct((INNER, SHOTS), BF16),
            jax.ShapeDtypeStruct((480, SHOTS), BF16),
        ),
        in_specs=[vmem] * 2,
        out_specs=(pl.BlockSpec(memory_space=pltpu.HBM),) * 2,
        scratch_shapes=[dma((2,))],
        compiler_params=pltpu.CompilerParams(vmem_limit_bytes=8 * 1024 * 1024),
    )(inner, sep)
    return inner[None, None], sep[None, None]


def solution(mesh):
    leaf, factor = P("sub", "sep", None, None), P("sub", "sep", None)
    return jax.shard_map(
        local,
        mesh=mesh,
        in_specs=(leaf, leaf, leaf, factor) + (factor,) * 7,
        out_specs=(leaf, leaf),
        check_vma=False,
    )
```

time: 47.5 us -> 41.5 us (0.87)
  local copies, waits for them, and re-layouts: 3.42 us -> 0 us
  Pallas kernels: 43.2 us -> 40.8 us
    unnamed x2 -> x0, local copies, waits for them, and re-layouts: 3.42 us -> none
    pallas_call x1, Pallas kernels: 43.2 us -> 39.9 us  [local(): pl.pallas_call(kernel, out_shape=(jax.ShapeDtypeStruct((INNER, SHOTS), BF...]
    pallas_call x0 -> x1, Pallas kernels: none -> 0.84 us  [local(): pl.pallas_call(write_out, out_shape=(jax.ShapeDtypeStruct((INNER, SHOTS),...]
where the time goes in v2:
time: 41.5 us; the launch traced here: 41.4 us
  Pallas kernels  40.8 us (98%)
  between operations  0.64 us (2%)
    pallas_call x1, Pallas kernels, local(): pl.pallas_call(kernel, out_shape=(jax.ShapeDtypeStruct((INNER, SHOTS), BF...  39.9 us
    pallas_call x1, Pallas kernels, local(): pl.pallas_call(write_out, out_shape=(jax.ShapeDtypeStruct((INNER, SHOTS),...  0.84 us

profile of v2, /device:TPU:1, one launch (start us, length us, event | category | flops | bytes accessed | tf_op | source)
XLA Modules:
  0.0 41.4 jit_solution(17010571905254328560)
XLA Ops:
  0.6 39.9 %shard_map.122 = (bf16[768,256]{1,0:T(8,128)(2,1)S(1)}, bf16[480,256]{1,0:T(8,128)(2,1)S(1)}) custom-call(bf16[768,256]{1,0:T(8,128)(2,1)} %bitcast.15, bf16[768,768]{1,0:T(8,128)(2,1)} %bitcast.13, bf16[512,768]{1,0:T(8,128)(2,1)} %bitcast.14, s32[1,512]{1,0:T(1,128)} %bitcast.23, bf16[32,64]{1,0:T(8,128)(2,1)} %bitcast.22, bf16[64,128]{1,0:T(8,128)(2,1)} %bitcast.20, ...), custom_call_target="tpu_custom_call" | custom-call | tf_op jit(solution)/shard_map/pallas_call | solution.py:349
  40.6 0.8 %shard_map.123 = (bf16[768,256]{1,0:T(8,128)(2,1)}, bf16[480,256]{1,0:T(8,128)(2,1)}) custom-call(bf16[768,256]{1,0:T(8,128)(2,1)S(1)} %get-tuple-element.6.inner, bf16[480,256]{1,0:T(8,128)(2,1)S(1)} %get-tuple-element.7.sep), custom_call_target="tpu_custom_call" | custom-call | tf_op jit(solution)/shard_map/pallas_call | solution.py:362

commit v3 on v2

--- a/solution.py
+++ b/solution.py
@@ -39,8 +39,8 @@
     inner_ref, sep_ref,
     src, a, cm, mp, s0, s1, s2, s3, k0, k1, k2,
     ih, lt3, ltr, p3, pr, w, xb, yb, e1, e2, g1, g2, g3, nn, direct,
-    v3, v2, v1, b3, b2, b1, t3, t2, h3, h2, r3, r2, o3, orr, d3a, dra,
-    load_sem, fac_s, fac_r, p1_s, p1_r, p2_s, p2_r, p3_s, p3_r, p4_s, p4_r, p5_s, p5_r,
+    tl, q3, v3, v2, v1, b3, b2, b1, t3, t2, h3, h2, r3, r2, o3, orr, d3a, dra,
+    far_sem, load_sem, fac_s, fac_r, p1_s, p1_r, p2_s, p2_r, p3_s, p3_r, p4_s, p4_r, p5_s, p5_r,
 ):
     sub = lax.axis_index("sub")
     core = lax.axis_index("sep")
@@ -71,9 +71,11 @@
     ring = [4, 3, 5, 2, 6, 1, 7]
 
     barrier = pltpu.get_barrier_semaphore()
-    peers = [at(x, y, z_peer(j), core) for j in ring]
-    peers += [at(x, y_peer(j), z, core) for j in ring]
-    peers += [at(x_peer(dx, dc)[0], y, z, x_peer(dx, dc)[1]) for dx, dc in lines]
+    near = [2, 6, 1, 7]
+    peers = [at(x_peer(dx, dc)[0], y, z, x_peer(dx, dc)[1]) for dx, dc in lines[:2]]
+    peers += [at(x, y, z_peer(j), core) for j in near]
+    peers += [at(x, y_peer(j), z, core) for j in near]
+    peers += [at(x_peer(dx, dc)[0], y, z, x_peer(dx, dc)[1]) for dx, dc in lines[2:]]
     for peer in peers:
         pl.semaphore_signal(barrier, inc=1, device_id=peer, device_id_type=MESH)
 
@@ -118,6 +120,8 @@
     lt3[...] = mm_nt(bht, onehot[:256, :]).astype(BF16).reshape(X * C, OWN, 256)
     for copy in one[7:]:
         copy.start()
+    for peer in [at(x, y, z_peer(2), core), at(x, y, z_peer(6), core), at(x, y_peer(2), z, core), at(x, y_peer(6), z, core)]:
+        pl.semaphore_signal(far_sem, inc=1, device_id=peer, device_id_type=MESH)
     fac_copies = [
         send(h, v.at[core], fac_s.at[i], fac_r.at[i], at(x, y, z, 1 - core)) for i, (h, v) in enumerate(facs)
     ]
@@ -156,18 +160,24 @@
 
     for copy in one[:7]:
         copy.wait_recv()
-    rest = [line_sum(pr, p) for p in range(2)]
-    tails = jnp.concatenate([rest[0][:, 128:], rest[1][:, 128:]], axis=1).astype(BF16)
-    x1h = mm(tails, w[...]).astype(BF16)
-    x2 = jnp.concatenate([rest[0][:, :128], rest[1][:, :128]], axis=1) + mm_nt(x1h, e1[...])
-    x2h = x2.astype(BF16)
-    x3 = mm_nt(x2h, e2[...])
-    for k in range(4):
-        v2[k] = x2h[16 * (k // 2) : 16 * (k // 2) + 16, 128 * (k % 2) : 128 * (k % 2) + 128]
-    v1[...] = x1h
+
+    @pl.when(sub >= 0)
+    def _():
+        rest = [line_sum(pr, p) for p in range(2)]
+        tails = jnp.concatenate([rest[0][:, 128:], rest[1][:, 128:]], axis=1).astype(BF16)
+        tl[...] = tails
+        x1h = mm(tails, w[...]).astype(BF16)
+        x2 = jnp.concatenate([rest[0][:, :128], rest[1][:, :128]], axis=1) + mm_nt(x1h, e1[...])
+        x2h = x2.astype(BF16)
+        q3[...] = mm_nt(x2h, e2[...])
+        for k in range(4):
+            v2[k] = x2h[16 * (k // 2) : 16 * (k // 2) + 16, 128 * (k % 2) : 128 * (k % 2) + 128]
+        v1[...] = x1h
+
+    pl.semaphore_wait(far_sem, 4)
     for copy in one[7:]:
         copy.wait_recv()
-    x3h = (x3 + jnp.concatenate([line_sum(p3, 0), line_sum(p3, 1)], axis=1)).astype(BF16)
+    x3h = (q3[...] + jnp.concatenate([line_sum(p3, 0), line_sum(p3, 1)], axis=1)).astype(BF16)
     for k in range(8):
         v3[k] = x3h[16 * (k // 4) : 16 * (k // 4) + 16, 128 * (k % 4) : 128 * (k % 4) + 128]
 
@@ -228,6 +238,8 @@
         nn[lo:hi, :] = mm(picked_rows[:, lo:], a[lo:, lo:hi]).T.astype(BF16)
     out_slot = lax.broadcasted_iota(jnp.int32, (480, WIDE), 0)
     nn[INNER:, :] = (slots((480, WIDE), 1) == out_slot).astype(BF16)
+    for copy in fac_copies + one + two:
+        copy.wait_send()
 
     for copy in three[:7]:
         copy.wait_recv()
@@ -252,7 +264,9 @@
     for j in range(1, 4):
         low = low + b1[j].astype(F32)
     own1 = mm(low.astype(BF16), g1[...])
-    own0 = mm(tails, yb[...])
+    own0 = mm(tl[...], yb[...])
+    for copy in three:
+        copy.wait_send()
     for copy in four[7:]:
         copy.wait_recv()
     whole2 = jnp.concatenate(
@@ -299,7 +313,7 @@
         lo, hi = 256 * i, 256 * (i + 1)
         inner_ref[lo:hi, :] = (direct[lo:hi, :] - mm_nt(nn[lo:hi, 256:], downr)).astype(BF16)
     sep_ref[:224, :] = mm_nt(nn[INNER : INNER + 224, 256:], downr).astype(BF16)
-    for copy in fac_copies + one + two + three + four + five:
+    for copy in four + five:
         copy.wait_send()
 
 
@@ -338,12 +352,13 @@
         v((256, 128), BF16), v((512, 256), BF16),
         v((128, 128), BF16), v((256, 256), BF16), v((512, 512), BF16),
         v((INNER + 480, WIDE), BF16), v((INNER, SHOTS), F32),
+        v((OWN, 256), BF16), v((OWN, WIDE), F32),
         v((8, 16, 128), BF16), v((4, 16, 128), BF16), v((32, 128), BF16),
         v((8, 16, 128), BF16), v((8, 16, 128), BF16), v((4, 32, 128), BF16),
         v((16, 128), BF16), v((16, 128), BF16), v((8, 16, 128), BF16), v((16, 128), BF16),
         v((8, 16, 128), BF16), v((4, 16, 128), BF16),
         v((2, OWN, 256), BF16), v((2, OWN, 256), BF16), piece, piece,
-        dma((13,)), dma((7,)), dma((7,)), dma((14,)), dma((14,)), dma((20,)), dma((20,)),
+        pltpu.SemaphoreType.REGULAR, dma((13,)), dma((7,)), dma((7,)), dma((14,)), dma((14,)), dma((20,)), dma((20,)),
         dma((9,)), dma((9,)), dma((12,)), dma((12,)), dma((14,)), dma((14,)),
     ]
     inner, sep = pl.pallas_call(

time: 41.5 us -> 40 us (0.964)
  Pallas kernels: 40.8 us -> 39.2 us
    pallas_call x1, Pallas kernels: 39.9 us -> 38.3 us  [local(): pl.pallas_call(kernel, out_shape=(jax.ShapeDtypeStruct((INNER, SHOTS), BF...]
where the time goes in v3:
time: 40 us; the launch traced here: 39.8 us
  Pallas kernels  39.2 us (98%)
  between operations  0.64 us (2%)
    pallas_call x1, Pallas kernels, local(): pl.pallas_call(kernel, out_shape=(jax.ShapeDtypeStruct((INNER, SHOTS), BF...  38.3 us
    pallas_call x1, Pallas kernels, local(): pl.pallas_call(write_out, out_shape=(jax.ShapeDtypeStruct((INNER, SHOTS),...  0.84 us

profile of v3, /device:TPU:1, one launch (start us, length us, event | category | flops | bytes accessed | tf_op | source)
XLA Modules:
  0.0 39.8 jit_solution(8317458512985617367)
XLA Ops:
  0.6 38.3 %shard_map.122 = (bf16[768,256]{1,0:T(8,128)(2,1)S(1)}, bf16[480,256]{1,0:T(8,128)(2,1)S(1)}) custom-call(bf16[768,256]{1,0:T(8,128)(2,1)} %bitcast.15, bf16[768,768]{1,0:T(8,128)(2,1)} %bitcast.13, bf16[512,768]{1,0:T(8,128)(2,1)} %bitcast.14, s32[1,512]{1,0:T(1,128)} %bitcast.23, bf16[32,64]{1,0:T(8,128)(2,1)} %bitcast.22, bf16[64,128]{1,0:T(8,128)(2,1)} %bitcast.20, ...), custom_call_target="tpu_custom_call" | custom-call | tf_op jit(solution)/shard_map/pallas_call | solution.py:364
  39.0 0.8 %shard_map.123 = (bf16[768,256]{1,0:T(8,128)(2,1)}, bf16[480,256]{1,0:T(8,128)(2,1)}) custom-call(bf16[768,256]{1,0:T(8,128)(2,1)S(1)} %get-tuple-element.6.inner, bf16[480,256]{1,0:T(8,128)(2,1)S(1)} %get-tuple-element.7.sep), custom_call_target="tpu_custom_call" | custom-call | tf_op jit(solution)/shard_map/pallas_call | solution.py:377

commit v4 on v3

--- a/solution.py
+++ b/solution.py
@@ -107,6 +107,7 @@
     bh = mm(cm[...], ih[...])
     bht = bh.T.astype(BF16)
     ltr[...] = mm_nt(bht, onehot[256:, :]).astype(BF16).reshape(X * C, OWN, 256)
+    lt3[...] = mm_nt(bht, onehot[:256, :]).astype(BF16).reshape(X * C, OWN, 256)
     pl.semaphore_wait(barrier, len(peers))
 
     one = []
@@ -117,7 +118,6 @@
             one.append(send(source.at[xx * C + cc], target.at[own], p1_s.at[k], p1_r.at[k], at(xx, y, z, cc)))
     for copy in one[:7]:
         copy.start()
-    lt3[...] = mm_nt(bht, onehot[:256, :]).astype(BF16).reshape(X * C, OWN, 256)
     for copy in one[7:]:
         copy.start()
     for peer in [at(x, y, z_peer(2), core), at(x, y, z_peer(6), core), at(x, y_peer(2), z, core), at(x, y_peer(6), z, core)]:
@@ -161,7 +161,7 @@
     for copy in one[:7]:
         copy.wait_recv()
 
-    @pl.when(sub >= 0)
+    @pl.when(sub < X * Y * Z)
     def _():
         rest = [line_sum(pr, p) for p in range(2)]
         tails = jnp.concatenate([rest[0][:, 128:], rest[1][:, 128:]], axis=1).astype(BF16)
@@ -193,19 +193,21 @@
     for copy in two[:14]:
         copy.start()
 
-    g0 = mm_tn(f0, f0).astype(BF16)
-    g1[...] = mm_tn(f1, f1).astype(BF16)
-    g2[...] = mm_tn(f2, f2).astype(BF16)
-    g3[...] = mm_tn(f3, f3).astype(BF16)
-    yb[...] = jnp.zeros_like(yb)
-    blank = jnp.zeros((32, 64), BF16)
-    gap = jnp.zeros((32, 32), BF16)
-    for p in range(2):
-        rows = g0[32 * p : 32 * p + 32, :]
-        yb[128 * p + 64 : 128 * p + 96, :] = jnp.concatenate([blank, rows[:, :32], gap, blank, rows[:, 32:], gap], axis=1)
-    wt = w[...].astype(F32).T
-    lane = lax.rem(lax.broadcasted_iota(jnp.int32, (128, 256), 1), 128)
-    xb[...] = jnp.where(lane < 64, wt, -wt).astype(BF16)
+    @pl.when(sub < X * Y * Z)
+    def _():
+        g0 = mm_tn(f0, f0).astype(BF16)
+        g1[...] = mm_tn(f1, f1).astype(BF16)
+        g2[...] = mm_tn(f2, f2).astype(BF16)
+        g3[...] = mm_tn(f3, f3).astype(BF16)
+        yb[...] = jnp.zeros_like(yb)
+        blank = jnp.zeros((32, 64), BF16)
+        gap = jnp.zeros((32, 32), BF16)
+        for p in range(2):
+            rows = g0[32 * p : 32 * p + 32, :]
+            yb[128 * p + 64 : 128 * p + 96, :] = jnp.concatenate([blank, rows[:, :32], gap, blank, rows[:, 32:], gap], axis=1)
+        wt = w[...].astype(F32).T
+        lane = lax.rem(lax.broadcasted_iota(jnp.int32, (128, 256), 1), 128)
+        xb[...] = jnp.where(lane < 64, wt, -wt).astype(BF16)
 
     for copy in two[:7]:
         copy.wait_recv()

time: 40 us -> 39.7 us (level)
  no operation moved by 1% of the time
where the time goes in v4:
time: 39.7 us; the launch traced here: 39.6 us
  Pallas kernels  38.9 us (98%)
  between operations  0.64 us (2%)
    pallas_call x1, Pallas kernels, local(): pl.pallas_call(kernel, out_shape=(jax.ShapeDtypeStruct((INNER, SHOTS), BF...  38.1 us
    pallas_call x1, Pallas kernels, local(): pl.pallas_call(write_out, out_shape=(jax.ShapeDtypeStruct((INNER, SHOTS),...  0.84 us

profile of v4, /device:TPU:1, one launch (start us, length us, event | category | flops | bytes accessed | tf_op | source)
XLA Modules:
  0.0 39.6 jit_solution(455280288835953813)
XLA Ops:
  0.6 38.1 %shard_map.122 = (bf16[768,256]{1,0:T(8,128)(2,1)S(1)}, bf16[480,256]{1,0:T(8,128)(2,1)S(1)}) custom-call(bf16[768,256]{1,0:T(8,128)(2,1)} %bitcast.15, bf16[768,768]{1,0:T(8,128)(2,1)} %bitcast.13, bf16[512,768]{1,0:T(8,128)(2,1)} %bitcast.14, s32[1,512]{1,0:T(1,128)} %bitcast.23, bf16[32,64]{1,0:T(8,128)(2,1)} %bitcast.22, bf16[64,128]{1,0:T(8,128)(2,1)} %bitcast.20, ...), custom_call_target="tpu_custom_call" | custom-call | tf_op jit(solution)/shard_map/pallas_call | solution.py:366
  38.7 0.8 %shard_map.123 = (bf16[768,256]{1,0:T(8,128)(2,1)}, bf16[480,256]{1,0:T(8,128)(2,1)}) custom-call(bf16[768,256]{1,0:T(8,128)(2,1)S(1)} %get-tuple-element.6.inner, bf16[480,256]{1,0:T(8,128)(2,1)S(1)} %get-tuple-element.7.sep), custom_call_target="tpu_custom_call" | custom-call | tf_op jit(solution)/shard_map/pallas_call | solution.py:379
